TPU v7x, 128 devices: a whole 4x4x4 slice. The times are simulated.
128 devices in a mesh: seq: 16 (over y, z_lo, core), tp: 8 (over z_hi, x).
Axes of the slice: x: 4, y: 4, z: 4 (z_hi: 2, z_lo: 2; z = z_hi * 2 + z_lo), core: 2. Of those that a mesh axis runs over, the one named last changes fastest.
Arguments:
- tokens: bfloat16 [8192, 2048], P('seq'), may hold values from -6 to 6
- w_zx: float32 [2048, 8192], P(('seq', 'tp')), may hold values from -0.125 to 0.125
- w_dt: float32 [2048, 64], P(('seq', 'tp')), may hold values from -0.26516503 to 0.26516503
- w_bc: float32 [2048, 256], P(('seq', 'tp')), may hold values from -0.125 to 0.125
- conv_x_weight: float32 [4, 4096], P(None, 'tp'), may hold values from -3 to 3
- conv_x_bias: float32 [4096], P('tp'), may hold values from -1.8 to 1.8
- conv_bc_weight: float32 [4, 256], replicated, may hold values from -3 to 3
- conv_bc_bias: float32 [256], replicated, may hold values from -1.8 to 1.8
- dt_bias: float32 [64], P('tp'), may hold values from -11 to -2
- a_log: float32 [64], P('tp'), may hold values from 0 to 2.77
- skip: float32 [64], P('tp'), may hold values from 0.5 to 2
- norm_weight: float32 [4096], P('tp'), may hold values from 0.1 to 1.9
- w_out: float32 [4096, 2048], P('tp', 'seq'), may hold values from -0.09375 to 0.09375
- lengths: int32 [8], replicated, may hold values from 1 to 4096, 8192 in all
- request_group: int32 [32], replicated, may hold values from 0 to 31
Outputs:
- mixed: bfloat16 [8192, 2048], P(('seq', 'tp'))
- request_states: float32 [32, 64, 64, 128], P('seq', 'tp')
Inputs may be any that keep to these rules, and one draw needn't show every extreme that they name: 8 prompts packed end to end in this order; the lengths sum to 8192 and the longest is exactly 4096.
All inputs are finite; a program needn't handle non-finite values.
Results may differ from a plain program's by a relative error of at most 0.011.
Values may be sent and summed in bfloat16 or wider, within the bound.
A program may use at most 128 MiB of HBM per device.

v0:
```python
import jax
import jax.numpy as jnp
from jax import lax
from jax.sharding import PartitionSpec as P

INNER = 4096
GROUP = 256
epsilon = 1e-05


def from_behind(x, axis, by):
    count = lax.axis_size(axis)
    pairs = [(i, i + by) for i in range(count) if 0 <= i + by < count]
    return lax.ppermute(x, axis, pairs)


def segment_of(position, lengths):
    prompt_ends = jnp.cumsum(lengths)
    return jnp.sum((position[:, None] >= prompt_ends[None, :]).astype(jnp.int32), axis=1)


def round_up(n, m):
    return (n + m - 1) // m * m


def on_device(
    tokens,
    w_zx,
    w_dt,
    w_bc,
    conv_x_weight,
    conv_x_bias,
    conv_bc_weight,
    conv_bc_bias,
    dt_bias,
    a_log,
    skip,
    norm_weight,
    w_out,
    lengths,
    request_group,
):
    tp_count = lax.axis_size("tp")
    seq_count = lax.axis_size("seq")
    seq_index = lax.axis_index("seq")
    tok_dev = tokens.shape[0]
    local_rows = w_zx.shape[0]
    inner_local = conv_x_weight.shape[1]
    heads_local = dt_bias.shape[0]
    head_width = inner_local // heads_local
    bc_width = conv_bc_weight.shape[1]
    state_width = bc_width // 2
    taps = conv_x_weight.shape[0]
    groups_dev = tok_dev // GROUP
    zx_part = w_zx.astype(jnp.bfloat16).reshape(local_rows, 2, tp_count, inner_local)
    zx_part = zx_part.transpose(0, 2, 1, 3).reshape(local_rows, tp_count, 2 * inner_local)
    bc_part = jnp.broadcast_to(
        w_bc.astype(jnp.bfloat16)[:, None, :], (local_rows, tp_count, bc_width)
    )
    dt_part = w_dt.astype(jnp.bfloat16).reshape(local_rows, tp_count, heads_local)
    used = 2 * inner_local + bc_width + heads_local
    width = round_up(used, 128)
    pad_part = jnp.zeros((local_rows, tp_count, width - used), jnp.bfloat16)
    packed = jnp.concatenate([zx_part, bc_part, dt_part, pad_part], axis=2)
    packed = packed.reshape(local_rows, tp_count * width)
    block = lax.all_to_all(packed, "tp", split_axis=1, concat_axis=0, tiled=True)
    weights = lax.all_gather(block, "seq", axis=0, tiled=True)
    proj = jnp.dot(tokens, weights, preferred_element_type=jnp.float32)
    zx_low = proj[:, : 2 * inner_local].astype(jnp.bfloat16)
    gate_z = zx_low[:, :inner_local]
    x_raw = zx_low[:, inner_local:]
    bc_raw = proj[:, 2 * inner_local : 2 * inner_local + bc_width].astype(jnp.bfloat16)
    dt_pre = proj[:, 2 * inner_local + bc_width : used]
    raw_mix = jnp.concatenate([x_raw, bc_raw], axis=1)
    conv_weight = jnp.concatenate([conv_x_weight, conv_bc_weight], axis=1)
    conv_bias = jnp.concatenate([conv_x_bias, conv_bc_bias], axis=0)
    rim_rows = from_behind(raw_mix[tok_dev - (taps - 1) :], "seq", 1)
    padded = jnp.concatenate([rim_rows, raw_mix], axis=0)
    offset = seq_index * tok_dev
    seg_pad = segment_of(
        offset - (taps - 1) + jnp.arange(tok_dev + taps - 1, dtype=jnp.int32), lengths
    )
    seg_tok = seg_pad[taps - 1 :]
    conv_sum = jnp.zeros((tok_dev, raw_mix.shape[1]), jnp.float32) + conv_bias[None, :]
    for offset_tap in range(taps):
        rows_wide = padded[offset_tap : offset_tap + tok_dev].astype(jnp.float32)
        keep_tap = seg_pad[offset_tap : offset_tap + tok_dev] == seg_tok
        conv_sum = conv_sum + jnp.where(
            keep_tap[:, None], rows_wide * conv_weight[offset_tap][None, :], 0.0
        )
    convolved = jax.nn.silu(conv_sum).astype(jnp.bfloat16)
    inputs = convolved[:, :inner_local].reshape(groups_dev, GROUP, heads_local, head_width)
    b_matrix = convolved[:, inner_local : inner_local + state_width].reshape(
        groups_dev, GROUP, state_width
    )
    c_matrix = convolved[:, inner_local + state_width :].reshape(groups_dev, GROUP, state_width)
    step_size = jax.nn.softplus(dt_pre + dt_bias[None, :]).reshape(groups_dev, GROUP, heads_local)
    step_heads = step_size.transpose(0, 2, 1)
    decay_rate = -jnp.exp(a_log)
    cumul_heads = jnp.cumsum(step_size * decay_rate[None, None, :], axis=1).transpose(0, 2, 1)
    segments = seg_tok.reshape(groups_dev, GROUP)
    seg_before = segment_of(offset + jnp.arange(groups_dev, dtype=jnp.int32) * GROUP - 1, lengths)
    within = jnp.arange(GROUP, dtype=jnp.int32)
    same_prompt = (segments[:, :, None] == segments[:, None, :]) & (
        within[:, None] >= within[None, :]
    )[None]
    log_decay = cumul_heads[:, :, :, None] - cumul_heads[:, :, None, :]
    decay_matrix = jnp.where(
        same_prompt[:, None], jnp.exp(jnp.where(same_prompt[:, None], log_decay, 0.0)), 0.0
    )
    scores = jnp.einsum("cin,cjn->cij", c_matrix, b_matrix, preferred_element_type=jnp.float32)
    mix_weights = (decay_matrix * scores[:, None] * step_heads[:, :, None, :]).astype(jnp.bfloat16)
    diag_out = jnp.einsum(
        "chij,cjhp->cihp", mix_weights, inputs, preferred_element_type=jnp.float32
    )
    last_segment = segments[:, -1]
    tail_weight = (
        jnp.where(
            (segments == last_segment[:, None])[:, None, :],
            jnp.exp(cumul_heads[:, :, -1:] - cumul_heads),
            0.0,
        )
        * step_heads
    )
    b_weighted = (b_matrix.astype(jnp.float32)[:, None] * tail_weight[:, :, :, None]).astype(
        jnp.bfloat16
    )
    contrib = jnp.einsum("cjhp,chjn->chpn", inputs, b_weighted, preferred_element_type=jnp.float32)
    pass_gate = jnp.where(
        (last_segment == seg_before)[:, None], jnp.exp(cumul_heads[:, :, -1]), 0.0
    )

    def local_step(carry_state, group_item):
        factor, source = group_item
        next_state = factor[:, None, None] * carry_state + source
        return (next_state, (carry_state, next_state))

    zero_state = jnp.zeros((heads_local, head_width, state_width), jnp.float32)
    _, (local_in, local_end) = lax.scan(local_step, zero_state, (pass_gate, contrib))
    through_group = jnp.cumprod(pass_gate, axis=0)
    before_group = jnp.concatenate(
        [jnp.ones((1, heads_local), jnp.float32), through_group[:-1]], axis=0
    )
    gate_hi = through_group.astype(jnp.bfloat16)
    gate_lo = (through_group - gate_hi.astype(jnp.float32)).astype(jnp.bfloat16)
    extra = jnp.zeros((groups_dev, heads_local, 8, state_width), jnp.bfloat16)
    extra = extra.at[:, :, 0, :].set(
        jnp.broadcast_to(gate_hi[:, :, None], gate_hi.shape + (state_width,))
    )
    extra = extra.at[:, :, 1, :].set(
        jnp.broadcast_to(gate_lo[:, :, None], gate_lo.shape + (state_width,))
    )
    sendable = jnp.concatenate([local_end.astype(jnp.bfloat16), extra], axis=2)
    every = lax.all_gather(sendable, "seq", axis=0, tiled=False)
    every_end = every[:, :, :, :head_width].astype(jnp.float32)
    every_gate = every[:, :, :, head_width, 0].astype(jnp.float32) + every[
        :, :, :, head_width + 1, 0
    ].astype(jnp.float32)
    dev_gate = every_gate[:, -1]
    dev_ids = jnp.arange(seq_count, dtype=jnp.int32)

    def carry_weights(k):
        between = (dev_ids[:, None] < dev_ids[None, :]) & (dev_ids[None, :] < k)
        factors = jnp.where(between[:, :, None], dev_gate[None, :, :], 1.0)
        return jnp.where((dev_ids < k)[:, None], jnp.prod(factors, axis=1), 0.0)

    own_weights = carry_weights(seq_index)
    slot_ids = jnp.arange(groups_dev, dtype=jnp.int32)
    last_slot = (slot_ids == groups_dev - 1).astype(jnp.float32)
    own_coef = own_weights[:, None, :] * last_slot[None, :, None]
    carried = jnp.einsum(
        "jch,jchpn->hpn",
        own_coef,
        every_end,
        precision=lax.Precision.HIGHEST,
        preferred_element_type=jnp.float32,
    )
    group_in = before_group[:, :, None, None] * carried[None] + local_in
    state_low = group_in.astype(jnp.bfloat16)
    carry_keep = jnp.where((segments == seg_before[:, None])[:, None, :], jnp.exp(cumul_heads), 0.0)
    carry_out = jnp.einsum(
        "cin,chpn->cihp", c_matrix, state_low, preferred_element_type=jnp.float32
    )
    carry_out = carry_out * carry_keep.transpose(0, 2, 1)[:, :, :, None]
    y_local = diag_out + carry_out + skip[None, None, :, None] * inputs.astype(jnp.float32)
    y_local = y_local.reshape(tok_dev, inner_local)
    gated = y_local * jax.nn.silu(gate_z.astype(jnp.float32))
    square_sum = jnp.sum(gated * gated, axis=1)
    scaled = (gated * norm_weight[None, :]).astype(jnp.bfloat16)
    out_shard = w_out.astype(jnp.bfloat16)
    out_block = lax.all_gather(out_shard, "seq", axis=1, tiled=True)
    partial = jnp.dot(scaled, out_block, preferred_element_type=jnp.float32)
    side = jnp.zeros((tok_dev, 128), jnp.float32).at[:, 0].set(square_sum)
    summed = lax.psum_scatter(
        jnp.concatenate([partial, side], axis=1), "tp", scatter_dimension=0, tiled=True
    )
    d_model = out_block.shape[1]
    mean_square = summed[:, d_model] / INNER
    mixed = (summed[:, :d_model] * lax.rsqrt(mean_square + epsilon)[:, None]).astype(jnp.bfloat16)
    req_dev = request_group.shape[0] // seq_count
    mine = lax.dynamic_slice_in_dim(request_group, seq_index * req_dev, req_dev)
    req_k = mine // groups_dev
    req_c = mine % groups_dev
    req_w = jax.vmap(carry_weights)(req_k)
    req_gate = every_gate[req_k, req_c]
    coef = req_gate[:, None, None, :] * req_w[:, :, None, :] * last_slot[None, None, :, None]
    hit = (dev_ids[None, :, None] == req_k[:, None, None]) & (
        slot_ids[None, None, :] == req_c[:, None, None]
    )
    coef = coef + hit[:, :, :, None].astype(jnp.float32)
    request_states = jnp.einsum(
        "rjch,jchpn->rhpn",
        coef,
        every_end,
        precision=lax.Precision.HIGHEST,
        preferred_element_type=jnp.float32,
    )
    return (mixed.astype(jnp.bfloat16), request_states)


def solution(mesh):
    return jax.shard_map(
        on_device,
        mesh=mesh,
        in_specs=(
            P("seq", None),
            P(("seq", "tp"), None),
            P(("seq", "tp"), None),
            P(("seq", "tp"), None),
            P(None, "tp"),
            P("tp"),
            P(),
            P(),
            P("tp"),
            P("tp"),
            P("tp"),
            P("tp"),
            P("tp", "seq"),
            P(),
            P(),
        ),
        out_specs=(P(("seq", "tp"), None), P("seq", "tp", None, None)),
        check_vma=False,
    )
```

profile of v0, /device:TPU:0, one launch (start us, length us, event | category | flops | bytes accessed | tf_op | source)
XLA Modules:
  0.0 278.6 jit_solution(9809869660556258186)
XLA Ops:
  9.3 17.5 %all_to_all.16 = bf16[16,8,1408]{2,0,1:T(8,128)(2,1)} all-to-all(bf16[16,8,1408]{2,0,1:T(8,128)(2,1)S(1)} %concatenate.34), channel_id=1, replica_groups=mesh['seq'=16,'tp'=8] {'tp'}, dimensions={1} | all-to-all | bytes 720896 | tf_op jit(solution)/shard_map/all_to_all | solution.py:66
  30.0 35.2 %all-gather.5.cloned.1.call-done = bf16[2048,1408]{1,0:T(8,128)(2,1)} async-done(((bf16[128,1408]{1,0:T(8,128)(2,1)}), bf16[2048,1408]{1,0:T(8,128)(2,1)}) %all-gather.5.cloned.1.call-update) | async-done | bytes 5767184 | tf_op jit(solution)/shard_map/all_gather | solution.py:67
  65.2 6.9 %fusion.59 = (bf16[512,1408]{0,1:T(8,128)(2,1)}, f32[512,1408]{0,1:T(8,128)S(1)}) fusion(bf16[2048,1408]{1,0:T(8,128)(2,1)} %all-gather.5.cloned.1.call-done, bf16[512,2048]{1,0:T(8,128)(2,1)S(1)} %copy-done), kind=kOutput, calls=%fused_computation.139 | convolution fusion | flops 2953510912 | bytes 12189696 | tf_op jit(solution)/shard_map/dot_general | solution.py:68
  75.6 2.2 collective-permute-start
  81.7 1.4 scatter.11
  83.1 2.9 %multiply_convert_fusion.3 = bf16[512,768]{0,1:T(8,128)(2,1)S(1)} fusion(bf16[512,768]{0,1:T(8,128)(2,1)S(1)} %slice.195, bf16[3,768]{0,1:T(8,128)(2,1)S(1)} %collective-permute-done, f32[768]{0:T(1024)} %get-tuple-element.107, f32[768]{0:T(1024)} %get-tuple-element.108, f32[768]{0:T(1024)} %get-tuple-element.109, f32[768]{0:T(1024)} %get-tuple-element.106, ...), kind=kLoop, calls=%fused_computation.22 | loop fusion | flops 11403264 | bytes 1594368 | tf_op jit(solution)/shard_map/convert_element_type | solution.py:91
  88.6 2.0 fusion.22
  90.5 5.0 %while.18 = (s32[]{:T(128)}, f32[8,64,128]{2,1,0:T(8,128)S(1)}, f32[2,8,64,128]{3,2,1,0:T(8,128)}, bf16[2,8,64,128]{3,2,1,0:T(8,128)(2,1)}, f32[2,8]{1,0:T(2,128...) while((s32[]{:T(128)}, f32[8,64,128]{2,1,0:T(8,128)S(1)}, ...), condition=%wide.region_7.8_spmd.clone, body=%wide.region_6.7_spmd.clone.sunk | while | flops 196611 | bytes 1311907 | solution.py:139
  91.7 1.3 bitcast_dynamic-update-slice_fusion.3
  94.2 1.3 bitcast_dynamic-update-slice_fusion.3
  95.5 1.7 pad_maximum_fusion.1
  97.3 1.6 convert_element_type.144
  102.5 2.5 fusion.12
  105.1 31.7 %all-gather.9.cloned.1.call-done = bf16[32,8,72,128]{3,2,1,0:T(8,128)(2,1)} async-done(((bf16[2,8,72,128]{3,2,1,0:T(8,128)(2,1)}), bf16[32,8,72,128]{3,2,1,0:T(8,128)(2,1)}) %all-gather.9.cloned.1.call-update) | async-done | bytes 4718608 | tf_op jit(solution)/shard_map/all_gather | solution.py:154
  136.7 5.8 %slice.215 = bf16[16,2,8,64,128]{4,3,2,1,0:T(8,128)(2,1)} slice(bf16[16,2,8,72,128]{4,3,2,1,0:T(8,128)(2,1)} %bitcast.91), slice={[0:16], [0:2], [0:8], [0:64], [0:128]} | slice | bytes 8388608 | tf_op jit(solution)/shard_map/slice | solution.py:155
  142.5 1.5 fusion.57
  145.0 6.3 %fusion.3 = f32[8,1,64,128,1]{3,1,4,2,0:T(1,128)S(1)} fusion(f32[16,2,8,1,1]{0,3,1,4,2:T(1,128)S(1)} %copy.133, bf16[16,2,8,64,128]{4,3,2,1,0:T(8,128)(2,1)} %slice.215), kind=kOutput, calls=%fused_computation.11 | convolution fusion | flops 25165824 | bytes 4457472 | tf_op jit(solution)/shard_map/jch,jchpn->hpn/dot_general | solution.py:171
  152.6 1.4 multiply_reduce_fusion
  154.7 21.8 %all-gather.7.cloned.1.call-done = bf16[512,2048]{1,0:T(8,128)(2,1)} async-done(((bf16[512,128]{1,0:T(8,128)(2,1)}), bf16[512,2048]{1,0:T(8,128)(2,1)}) %all-gather.7.cloned.1.call-update) | async-done | bytes 2097168 | tf_op jit(solution)/shard_map/all_gather | solution.py:191
  176.5 3.2 %fusion.27 = f32[512,2048]{1,0:T(8,128)S(1)} fusion(bf16[512,2048]{1,0:T(8,128)(2,1)} %all-gather.7.cloned.1.call-done, f32[512]{0:T(512)S(1)} %copy-done.18, f32[512,512]{0,1:T(8,128)S(1)} %bitcast.94, bf16[512,1408]{0,1:T(8,128)(2,1)} %get-tuple-element.143), kind=kOutput, calls=%fused_computation.46 | convolution fusion | flops 1075838976 | bytes 7866368 | tf_op jit(solution)/shard_map/dot_general | solution.py:192
  179.7 2.4 select_maximum_fusion
  184.4 5.8 %fusion.15 = f32[2,8,64,128]{3,0,2,1:T(2,128)S(1)} fusion(bf16[16,2,8,64,128]{4,3,2,1,0:T(8,128)(2,1)} %slice.215, f32[2,16,2]{1,0,2:T(2,128)S(1)} %and_convert_fusion, f32[2,16,8]{1,0,2:T(2,128)S(1)} %copy.130, f32[2]{0:T(128)S(1)} %compare_convert_fusion), kind=kOutput, calls=%fused_computation.31 | convolution fusion | flops 50332672 | bytes 4719880 | tf_op jit(solution)/shard_map/rjch,jchpn->rhpn/dot_general | solution.py:211
  191.1 78.3 %reduce-scatter.2.cloned.1.call-done = f32[64,2176]{1,0:T(8,128)} async-done(((f32[512,2176]{1,0:T(8,128)}), f32[64,2176]{1,0:T(8,128)}) %reduce-scatter.2.cloned.1.call-update) | async-done | bytes 557072 | tf_op jit(solution)/shard_map/reduce_scatter | solution.py:194
  270.2 1.9 fusion.28
  (141 shorter events, 28.0 us)
Async XLA Ops:
  7.2 58.1 %copy-start = (bf16[512,2048]{1,0:T(8,128)(2,1)S(1)}, bf16[512,2048]{1,0:T(8,128)(2,1)}, u32[]{:S(2)}) copy-start(bf16[512,2048]{1,0:T(8,128)(2,1)} %param.23) | copy-start | bytes 6291460
  7.2 1.8 copy-start.7
  7.2 1.8 copy-start.8
  7.2 19.7 %copy-start.19 = (s32[8]{0:T(128)S(1)}, s32[8]{0:T(128)}, u32[]{:S(2)}) copy-start(s32[8]{0:T(128)} %param.36) | copy-start | bytes 100
  7.2 20.5 %copy-start.9 = (f32[4,512]{1,0:T(4,128)S(1)}, f32[4,512]{1,0:T(4,128)}, u32[]{:S(2)}) copy-start(f32[4,512]{1,0:T(4,128)} %param.27) | copy-start | bytes 24580
  7.2 20.6 %copy-start.10 = (f32[4,256]{1,0:T(4,128)S(1)}, f32[4,256]{1,0:T(4,128)}, u32[]{:S(2)}) copy-start(f32[4,256]{1,0:T(4,128)} %param.29) | copy-start | bytes 12292
  7.2 20.6 %copy-start.13 = (f32[512]{0:T(512)S(1)}, f32[512]{0:T(512)}, u32[]{:S(2)}) copy-start(f32[512]{0:T(512)} %param.28) | copy-start | bytes 6148
  7.2 20.6 %copy-start.14 = (f32[256]{0:T(256)S(1)}, f32[256]{0:T(256)}, u32[]{:S(2)}) copy-start(f32[256]{0:T(256)} %param.30) | copy-start | bytes 3076
  7.3 22.0 %copy-start.20 = (f32[8]{0:T(128)S(1)}, f32[8]{0:T(128)}, u32[]{:S(2)}) copy-start(f32[8]{0:T(128)} %param.32) | copy-start | bytes 100
  7.3 58.0 %all-gather.5.cloned.1.call-start = ((), (), s32[]{:S(2)}) async-start(), calls=%async_computation.2 | async-start | bytes 6127616 | tf_op jit(solution)/shard_map/all_gather | solution.py:67
  26.8 109.9 %all-gather.9.cloned.1.call-start = ((), (), s32[]{:S(2)}) async-start(), calls=%async_computation.5 | async-start | bytes 5013504 | tf_op jit(solution)/shard_map/all_gather | solution.py:154
  27.3 44.9 %copy-start.6 = (s32[2,256]{1,0:T(2,128)}, s32[2,256]{1,0:T(2,128)S(1)}, u32[]{:S(2)}) copy-start(s32[2,256]{1,0:T(2,128)S(1)} %eq.111) | copy-start | bytes 6148
  30.0 42.2 %copy-start.15 = (f32[8]{0:T(128)S(1)}, f32[8]{0:T(128)}, u32[]{:S(2)}) copy-start(f32[8]{0:T(128)} %param.31) | copy-start | bytes 100
  74.3 4.2 %copy-start.3 = (f32[2,8,256]{2,1,0:T(8,128)}, f32[2,8,256]{2,1,0:T(8,128)S(1)}, u32[]{:S(2)}) copy-start(f32[2,8,256]{2,1,0:T(8,128)S(1)} %get-tuple-element.130) | copy-start | bytes 49156
  75.6 7.5 %collective-permute-start = (bf16[3,768]{0,1:T(8,128)(2,1)S(1)}, bf16[3,768]{0,1:T(8,128)(2,1)S(1)}, u32[]{:S(2)}, u32[]{:S(2)}) collective-permute-start(bf16[3,768]{0,1:T(8,128)(2,1)S(1)} %slice.194), channel_id=1, source_target_pairs={{0,8},{8,16},{16,24},{24,32},{32,40},{40,48},{48,56},{56,64},{64,7... | collective-permute-start | bytes 13832 | tf_op jit(solution)/shard_map/ppermute | solution.py:14
  77.8 0.7 copy-start.12
  95.5 7.0 %copy-start.4 = (f32[2,8,256]{2,1,0:T(8,128)S(1)}, f32[2,8,256]{2,1,0:T(8,128)}, u32[]{:S(2)}) copy-start(f32[2,8,256]{2,1,0:T(8,128)} %copy-done.3) | copy-start | bytes 49156
  97.3 79.2 %all-gather.7.cloned.1.call-start = ((), (), s32[]{:S(2)}) async-start(), calls=%async_computation.3 | async-start | bytes 2228224 | tf_op jit(solution)/shard_map/all_gather | solution.py:191
  99.0 170.4 %reduce-scatter.2.cloned.1.call-start = ((), (), s32[]{:S(2)}) async-start(), calls=%async_computation.4 | async-start | bytes 5013504 | tf_op jit(solution)/shard_map/reduce_scatter | solution.py:194
  145.0 6.3 %copy-start.1 = (f32[2,256,8,64]{1,3,2,0:T(8,128)S(1)}, f32[2,256,8,64]{1,3,2,0:T(8,128)}, u32[]{:S(2)}) copy-start(f32[2,256,8,64]{1,3,2,0:T(8,128)} %fusion.12) | copy-start | bytes 3145732
  145.0 6.3 %copy-start.2 = (f32[2,8,64,128]{3,2,1,0:T(8,128)S(1)}, f32[2,8,64,128]{3,2,1,0:T(8,128)}, u32[]{:S(2)}) copy-start(f32[2,8,64,128]{3,2,1,0:T(8,128)} %get-tuple-element.72) | copy-start | bytes 1572868
  145.0 6.3 %copy-start.5 = (f32[2,256,8]{1,2,0:T(8,128)S(1)}, f32[2,256,8]{1,2,0:T(8,128)}, u32[]{:S(2)}) copy-start(f32[2,256,8]{1,2,0:T(8,128)} %get-tuple-element.129) | copy-start | bytes 49156
  145.0 6.3 %copy-start.16 = (f32[8]{0:T(128)S(1)}, f32[8]{0:T(128)}, u32[]{:S(2)}) copy-start(f32[8]{0:T(128)} %param.33) | copy-start | bytes 100
  152.5 24.0 %copy-start.18 = (f32[512]{0:T(512)S(1)}, f32[512]{0:T(512)}, u32[]{:S(2)}) copy-start(f32[512]{0:T(512)} %param.34) | copy-start | bytes 6148
  (2 other events, 1.2 us)
Sparse Core Ops, SparseCore 0:
  26.9 38.2 all-gather.4
  97.4 39.2 all-gather.8
  138.9 37.5 all-gather.6
  182.2 87.1 reduce-scatter.1
where the time goes:
time: 280 us; the launch traced here: 279 us
  waiting for transfers between devices  167 us (60%)
  matrix products  28.2 us (10%)
  other arithmetic  25.1 us (9%)
  local copies, waits for them, and re-layouts  24.3 us (9%)
  blocking collectives  17.5 us (6%)
  between operations  14.2 us (5%)
    reduce_scatter x1, waiting for transfers between devices, on_device(): lax.psum_scatter(jnp.concatenate([partial, side], axis=1), 'tp', scatter_...  78.3 us
    all_gather x1, waiting for transfers between devices, on_device(): weights = lax.all_gather(block, 'seq', axis=0, tiled=True)  35.2 us
    all_gather x1, waiting for transfers between devices, on_device(): every = lax.all_gather(sendable, 'seq', axis=0, tiled=False)  31.7 us
    all_gather x1, waiting for transfers between devices, on_device(): out_block = lax.all_gather(out_shard, 'seq', axis=1, tiled=True)  21.8 us
    all_to_all x1, blocking collectives, on_device(): lax.all_to_all(packed, 'tp', split_axis=1, concat_axis=0, tiled=True)  17.5 us
    dot_general x1, matrix products, on_device(): proj = jnp.dot(tokens, weights, preferred_element_type=jnp.float32)  6.92 us
    dot_general x1, matrix products, on_device(): jnp.einsum('jch,jchpn->hpn', own_coef, every_end, precision=lax.Precision...  6.27 us
    dot_general x1, matrix products, on_device(): jnp.einsum('rjch,jchpn->rhpn', coef, every_end, precision=lax.Precision.H...  5.76 us
  transfers between devices with their start and end apart: 5, of which 4 were waited for; matrix products, arithmetic and copies ran while one was open for 15% of the time, Pallas kernels for 0%

commit v1 on v0

--- a/solution.py
+++ b/solution.py
@@ -2,6 +2,7 @@
 import jax.numpy as jnp
 from jax import lax
 from jax.sharding import PartitionSpec as P
+from jax.lax import all_to_all, psum
 
 INNER = 4096
 GROUP = 256
@@ -64,7 +65,7 @@
     packed = jnp.concatenate([zx_part, bc_part, dt_part, pad_part], axis=2)
     packed = packed.reshape(local_rows, tp_count * width)
     block = lax.all_to_all(packed, "tp", split_axis=1, concat_axis=0, tiled=True)
-    weights = lax.all_gather(block, "seq", axis=0, tiled=True)
+    weights = jnp.concatenate(all_to_all(jnp.stack([block] * psum(1, "seq")), "seq", 0, 0), axis=0)
     proj = jnp.dot(tokens, weights, preferred_element_type=jnp.float32)
     zx_low = proj[:, : 2 * inner_local].astype(jnp.bfloat16)
     gate_z = zx_low[:, :inner_local]

time: 280 us -> 335 us (1.20)
  waiting for transfers between devices: 167 us -> 215 us
  starting transfers between devices: 2.33 us -> 7.03 us
    all_to_all x0 -> x1, waiting for transfers between devices: none -> 78.7 us  [on_device(): all_to_all(jnp.stack([block] * psum(1, 'seq')), 'seq', 0, 0)]
    all_gather x1 -> x0, waiting for transfers between devices: 35.2 us -> none  [on_device(): weights = lax.all_gather(block, 'seq', axis=0, tiled=True)]
    all_to_all x0 -> x1, starting transfers between devices: none -> 5.22 us  [on_device(): all_to_all(jnp.stack([block] * psum(1, 'seq')), 'seq', 0, 0)]
    all_gather x1, waiting for transfers between devices: 31.7 us -> 35.9 us  [on_device(): every = lax.all_gather(sendable, 'seq', axis=0, tiled=False)]
  transfers between devices with their start and end apart: 5 -> 5, of which waited for: 4 -> 4; matrix products, arithmetic and copies ran while one was open for 15% -> 12% of each run, Pallas kernels for 0% -> 0%
where the time goes in v1:
time: 335 us; the launch traced here: 334 us
  waiting for transfers between devices  215 us (64%)
  matrix products  28.2 us (8%)
  local copies, waits for them, and re-layouts  27.5 us (8%)
  other arithmetic  25.1 us (7%)
  blocking collectives  17.4 us (5%)
  between operations  14.2 us (4%)
  starting transfers between devices  7.03 us (2%)
    all_to_all x1, waiting for transfers between devices, on_device(): all_to_all(jnp.stack([block] * psum(1, 'seq')), 'seq', 0, 0)  78.7 us
    reduce_scatter x1, waiting for transfers between devices, on_device(): lax.psum_scatter(jnp.concatenate([partial, side], axis=1), 'tp', scatter_...  78.3 us
    all_gather x1, waiting for transfers between devices, on_device(): every = lax.all_gather(sendable, 'seq', axis=0, tiled=False)  35.9 us
    all_gather x1, waiting for transfers between devices, on_device(): out_block = lax.all_gather(out_shard, 'seq', axis=1, tiled=True)  21.8 us
    all_to_all x1, blocking collectives, on_device(): lax.all_to_all(packed, 'tp', split_axis=1, concat_axis=0, tiled=True)  17.4 us
    dot_general x1, matrix products, on_device(): proj = jnp.dot(tokens, weights, preferred_element_type=jnp.float32)  6.94 us
  transfers between devices with their start and end apart: 5, of which 4 were waited for; matrix products, arithmetic and copies ran while one was open for 12% of the time, Pallas kernels for 0%

profile of v1, /device:TPU:0, one launch (start us, length us, event | category | flops | bytes accessed | tf_op | source)
XLA Modules:
  0.0 334.1 jit_solution(17920812780556188298)
XLA Ops:
  9.3 17.4 %all_to_all.18 = bf16[16,8,1408]{2,0,1:T(8,128)(2,1)S(1)} all-to-all(bf16[16,8,1408]{2,0,1:T(8,128)(2,1)S(1)} %concatenate.34), channel_id=1, replica_groups=mesh['seq'=16,'tp'=8] {'tp'}, dimensions={1} | all-to-all | bytes 720896 | tf_op jit(solution)/shard_map/all_to_all | solution.py:67
  26.6 3.2 stack.5
  29.8 5.2 %all-to-all-start.1 = ((bf16[16,128,1408]{2,1,0:T(8,128)(2,1)}), bf16[16,128,1408]{2,1,0:T(8,128)(2,1)}, u32[]{:S(2)}, u32[]{:S(2)}) async-start(bf16[16,128,1408]{2,1,0:T(8,128)(2,1)} %stack.5), calls=%async_computation.1 | async-start | bytes 11534336 | tf_op jit(solution)/shard_map/all_to_all | solution.py:68
  38.2 78.7 %all-to-all-done.1 = bf16[16,128,1408]{2,1,0:T(8,128)(2,1)} async-done(((bf16[16,128,1408]{2,1,0:T(8,128)(2,1)}), bf16[16,128,1408]{2,1,0:T(8,128)(2,1)}, u32[]{:S(2)}, u32[]{:S(2)}) %all-to-all-start.1) | async-done | bytes 5767200 | tf_op jit(solution)/shard_map/all_to_all | solution.py:68
  116.9 6.9 %fusion.59 = (bf16[512,1408]{0,1:T(8,128)(2,1)}, f32[512,1408]{0,1:T(8,128)S(1)}) fusion(bf16[2048,1408]{1,0:T(8,128)(2,1)} %bitcast.6, bf16[512,2048]{1,0:T(8,128)(2,1)S(1)} %copy-done), kind=kOutput, calls=%fused_computation.139 | convolution fusion | flops 2953510912 | bytes 12189696 | tf_op jit(solution)/shard_map/dot_general | solution.py:69
  127.3 1.7 collective-permute-start
  132.9 1.4 scatter.11
  134.3 2.9 multiply_convert_fusion.3
  139.8 2.0 fusion.22
  141.8 5.0 %while.18 = (s32[]{:T(128)}, f32[8,64,128]{2,1,0:T(8,128)S(1)}, f32[2,8,64,128]{3,2,1,0:T(8,128)}, bf16[2,8,64,128]{3,2,1,0:T(8,128)(2,1)}, f32[2,8]{1,0:T(2,128...) while((s32[]{:T(128)}, f32[8,64,128]{2,1,0:T(8,128)S(1)}, ...), condition=%wide.region_7.8_spmd.clone, body=%wide.region_6.7_spmd.clone.sunk | while | flops 196611 | bytes 1311907 | solution.py:140
  146.8 1.7 pad_maximum_fusion.1
  148.6 1.6 convert_element_type.144
  153.8 2.5 fusion.12
  156.3 35.9 %all-gather.6.cloned.1.call-done = bf16[32,8,72,128]{3,2,1,0:T(8,128)(2,1)} async-done(((bf16[2,8,72,128]{3,2,1,0:T(8,128)(2,1)}), bf16[32,8,72,128]{3,2,1,0:T(8,128)(2,1)}) %all-gather.6.cloned.1.call-update) | async-done | bytes 4718608 | tf_op jit(solution)/shard_map/all_gather | solution.py:155
  192.2 5.8 %slice.215 = bf16[16,2,8,64,128]{4,3,2,1,0:T(8,128)(2,1)} slice(bf16[16,2,8,72,128]{4,3,2,1,0:T(8,128)(2,1)} %bitcast.92), slice={[0:16], [0:2], [0:8], [0:64], [0:128]} | slice | bytes 8388608 | tf_op jit(solution)/shard_map/slice | solution.py:156
  197.9 1.5 fusion.57
  200.4 6.3 %fusion.3 = f32[8,1,64,128,1]{3,1,4,2,0:T(1,128)S(1)} fusion(f32[16,2,8,1,1]{0,3,1,4,2:T(1,128)S(1)} %copy.133, bf16[16,2,8,64,128]{4,3,2,1,0:T(8,128)(2,1)} %slice.215), kind=kOutput, calls=%fused_computation.11 | convolution fusion | flops 25165824 | bytes 4457472 | tf_op jit(solution)/shard_map/jch,jchpn->hpn/dot_general | solution.py:172
  208.0 1.4 multiply_reduce_fusion
  210.2 21.8 %all-gather.4.cloned.1.call-done = bf16[512,2048]{1,0:T(8,128)(2,1)} async-done(((bf16[512,128]{1,0:T(8,128)(2,1)}), bf16[512,2048]{1,0:T(8,128)(2,1)}) %all-gather.4.cloned.1.call-update) | async-done | bytes 2097168 | tf_op jit(solution)/shard_map/all_gather | solution.py:192
  231.9 3.2 fusion.27
  235.1 2.4 select_maximum_fusion
  239.9 5.8 %fusion.15 = f32[2,8,64,128]{3,0,2,1:T(2,128)S(1)} fusion(bf16[16,2,8,64,128]{4,3,2,1,0:T(8,128)(2,1)} %slice.215, f32[2,16,2]{1,0,2:T(2,128)S(1)} %and_convert_fusion, f32[2,16,8]{1,0,2:T(2,128)S(1)} %copy.130, f32[2]{0:T(128)S(1)} %compare_convert_fusion), kind=kOutput, calls=%fused_computation.31 | convolution fusion | flops 50332672 | bytes 4719880 | tf_op jit(solution)/shard_map/rjch,jchpn->rhpn/dot_general | solution.py:212
  246.5 78.3 %reduce-scatter.2.cloned.1.call-done = f32[64,2176]{1,0:T(8,128)} async-done(((f32[512,2176]{1,0:T(8,128)}), f32[64,2176]{1,0:T(8,128)}) %reduce-scatter.2.cloned.1.call-update) | async-done | bytes 557072 | tf_op jit(solution)/shard_map/reduce_scatter | solution.py:195
  325.7 1.9 fusion.28
  (141 shorter events, 30.6 us)
Async XLA Ops:
  7.2 109.8 %copy-start = (bf16[512,2048]{1,0:T(8,128)(2,1)S(1)}, bf16[512,2048]{1,0:T(8,128)(2,1)}, u32[]{:S(2)}) copy-start(bf16[512,2048]{1,0:T(8,128)(2,1)} %param.23) | copy-start | bytes 6291460
  7.2 1.7 copy-start.7
  7.2 1.7 copy-start.8
  29.8 5.3 %copy-start.19 = (s32[8]{0:T(128)S(1)}, s32[8]{0:T(128)}, u32[]{:S(2)}) copy-start(s32[8]{0:T(128)} %param.36) | copy-start | bytes 100
  29.8 6.2 %copy-start.9 = (f32[4,512]{1,0:T(4,128)S(1)}, f32[4,512]{1,0:T(4,128)}, u32[]{:S(2)}) copy-start(f32[4,512]{1,0:T(4,128)} %param.27) | copy-start | bytes 24580
  29.8 6.2 %copy-start.10 = (f32[4,256]{1,0:T(4,128)S(1)}, f32[4,256]{1,0:T(4,128)}, u32[]{:S(2)}) copy-start(f32[4,256]{1,0:T(4,128)} %param.29) | copy-start | bytes 12292
  29.8 6.2 %copy-start.13 = (f32[512]{0:T(512)S(1)}, f32[512]{0:T(512)}, u32[]{:S(2)}) copy-start(f32[512]{0:T(512)} %param.28) | copy-start | bytes 6148
  29.8 6.2 %copy-start.14 = (f32[256]{0:T(256)S(1)}, f32[256]{0:T(256)}, u32[]{:S(2)}) copy-start(f32[256]{0:T(256)} %param.30) | copy-start | bytes 3076
  29.8 7.6 %copy-start.20 = (f32[8]{0:T(128)S(1)}, f32[8]{0:T(128)}, u32[]{:S(2)}) copy-start(f32[8]{0:T(128)} %param.32) | copy-start | bytes 100
  29.8 87.1 %all-to-all-start.1 = ((bf16[16,128,1408]{2,1,0:T(8,128)(2,1)}), bf16[16,128,1408]{2,1,0:T(8,128)(2,1)}, u32[]{:S(2)}, u32[]{:S(2)}) async-start(bf16[16,128,1408]{2,1,0:T(8,128)(2,1)} %stack.5), calls=%async_computation.1 | async-start | bytes 11534336 | tf_op jit(solution)/shard_map/all_to_all | solution.py:68
  35.0 157.1 %all-gather.6.cloned.1.call-start = ((), (), s32[]{:S(2)}) async-start(), calls=%async_computation.5 | async-start | bytes 5013504 | tf_op jit(solution)/shard_map/all_gather | solution.py:155
  35.5 88.4 %copy-start.6 = (s32[2,256]{1,0:T(2,128)}, s32[2,256]{1,0:T(2,128)S(1)}, u32[]{:S(2)}) copy-start(s32[2,256]{1,0:T(2,128)S(1)} %eq.111) | copy-start | bytes 6148
  116.9 6.9 %copy-start.15 = (f32[8]{0:T(128)S(1)}, f32[8]{0:T(128)}, u32[]{:S(2)}) copy-start(f32[8]{0:T(128)} %param.31) | copy-start | bytes 100
  126.1 3.7 %copy-start.3 = (f32[2,8,256]{2,1,0:T(8,128)}, f32[2,8,256]{2,1,0:T(8,128)S(1)}, u32[]{:S(2)}) copy-start(f32[2,8,256]{2,1,0:T(8,128)S(1)} %get-tuple-element.130) | copy-start | bytes 49156
  127.3 7.0 %collective-permute-start = (bf16[3,768]{0,1:T(8,128)(2,1)S(1)}, bf16[3,768]{0,1:T(8,128)(2,1)S(1)}, u32[]{:S(2)}, u32[]{:S(2)}) collective-permute-start(bf16[3,768]{0,1:T(8,128)(2,1)S(1)} %slice.194), channel_id=1, source_target_pairs={{0,8},{8,16},{16,24},{24,32},{32,40},{40,48},{48,56},{56,64},{64,7... | collective-permute-start | bytes 13832 | tf_op jit(solution)/shard_map/ppermute | solution.py:15
  129.0 0.7 copy-start.12
  146.8 7.0 %copy-start.4 = (f32[2,8,256]{2,1,0:T(8,128)S(1)}, f32[2,8,256]{2,1,0:T(8,128)}, u32[]{:S(2)}) copy-start(f32[2,8,256]{2,1,0:T(8,128)} %copy-done.3) | copy-start | bytes 49156
  148.5 83.4 %all-gather.4.cloned.1.call-start = ((), (), s32[]{:S(2)}) async-start(), calls=%async_computation.3 | async-start | bytes 2228224 | tf_op jit(solution)/shard_map/all_gather | solution.py:192
  150.2 174.6 %reduce-scatter.2.cloned.1.call-start = ((), (), s32[]{:S(2)}) async-start(), calls=%async_computation.4 | async-start | bytes 5013504 | tf_op jit(solution)/shard_map/reduce_scatter | solution.py:195
  200.4 6.3 %copy-start.1 = (f32[2,256,8,64]{1,3,2,0:T(8,128)S(1)}, f32[2,256,8,64]{1,3,2,0:T(8,128)}, u32[]{:S(2)}) copy-start(f32[2,256,8,64]{1,3,2,0:T(8,128)} %fusion.12) | copy-start | bytes 3145732
  200.4 6.3 %copy-start.2 = (f32[2,8,64,128]{3,2,1,0:T(8,128)S(1)}, f32[2,8,64,128]{3,2,1,0:T(8,128)}, u32[]{:S(2)}) copy-start(f32[2,8,64,128]{3,2,1,0:T(8,128)} %get-tuple-element.72) | copy-start | bytes 1572868
  200.4 6.3 %copy-start.5 = (f32[2,256,8]{1,2,0:T(8,128)S(1)}, f32[2,256,8]{1,2,0:T(8,128)}, u32[]{:S(2)}) copy-start(f32[2,256,8]{1,2,0:T(8,128)} %get-tuple-element.129) | copy-start | bytes 49156
  200.4 6.3 %copy-start.16 = (f32[8]{0:T(128)S(1)}, f32[8]{0:T(128)}, u32[]{:S(2)}) copy-start(f32[8]{0:T(128)} %param.33) | copy-start | bytes 100
  207.9 24.0 %copy-start.18 = (f32[512]{0:T(512)S(1)}, f32[512]{0:T(512)}, u32[]{:S(2)}) copy-start(f32[512]{0:T(512)} %param.34) | copy-start | bytes 6148
  (2 other events, 1.2 us)
Sparse Core Ops, SparseCore 0:
  148.6 43.4 all-gather.5
  194.4 37.5 all-gather.3
  237.6 87.1 reduce-scatter.1
